TPU v7x, 32 devices: a whole 2x2x4 slice. The times are simulated.
32 devices in a mesh: head: 2 (over core), seq: 16 (over z, y, x).
Axes of the slice: x: 2, y: 2, z: 4, core: 2. Of those that a mesh axis runs over, the one named last changes fastest.
Arguments:
- queries: bfloat16 [8192, 5120], P(('seq', 'head')), may hold values from -8 to 8
- key_states: bfloat16 [8192, 5120], P(('seq', 'head')), may hold values from -8 to 8
- value_states: bfloat16 [8192, 5120], P(('seq', 'head')), may hold values from -6 to 6
- cluster_perm: int32 [40, 8192], P('head', 'seq'), may hold values from 0 to 8191, as said below
- block_mask: int32 [40, 64, 64], P('head', 'seq'), may hold values from 0 to 1, as said below
Outputs:
- attention_out: bfloat16 [8192, 5120], P(('seq', 'head'))
Inputs may be any that keep to these rules, and one draw needn't show every extreme that they name: `cluster_perm`: for each head, positions k * 512 to (k + 1) * 512 - 1 list the tokens k * 512 to (k + 1) * 512 - 1, each once. `block_mask`: for each head and each aligned run of 4 query blocks, the key blocks used by some query block of the run number exactly 1. For such a run and the 20 heads g * 20 to (g + 1) * 20 - 1, the (head, key block) pairs so used that lie in one aligned run of 4 key blocks number at most 2, and exactly 2 in some run. Every query block uses 1 to 1 key blocks, and some query block of every run uses 1, for every head.
All inputs are finite; a program needn't handle non-finite values.
Results may differ from a plain program's by a relative error of at most 0.0049.
Values may be sent and summed in bfloat16 or wider, within the bound.
A program may use at most 128 MiB of HBM per device.

v0:
```python
import functools
import math

import jax
import jax.numpy as jnp
from jax import lax
from jax.experimental import pallas as pl
from jax.experimental.pallas import tpu as pltpu
from jax.sharding import PartitionSpec as P

HEAD_DIM = 128
BLOCK = 128
MESH = pl.DeviceIdType.MESH
HIGHEST = lax.Precision.HIGHEST


def iota(shape, dim):
    return lax.broadcasted_iota(jnp.int32, shape, dim)


def partner_of(me, step, count):
    if count & (count - 1):
        raise ValueError("seq size")
    peer = 0
    bit = 1
    while bit < count:
        peer = peer + bit * (((me // bit) + (step // bit)) % 2)
        bit *= 2
    return peer


def route(shard_blocks, capacity, picks, mask_ref, req_ref, pos_ref):
    heads, _, blocks = mask_ref.shape
    seq_count = blocks // shard_blocks
    needed = jnp.max(mask_ref[...], axis=1).astype(jnp.float32)
    row, col = iota((blocks, blocks), 0), iota((blocks, blocks), 1)
    same = (row // shard_blocks) == (col // shard_blocks)
    dot = functools.partial(jnp.dot, precision=HIGHEST, preferred_element_type=jnp.float32)
    ones = lambda flag: flag.astype(jnp.float32)
    by_owner = dot(needed, ones(same))
    before_in_owner = dot(needed, ones(same & (row < col)))
    before_all = dot(needed, ones(row < col))
    lower = ones(iota((heads, heads), 1) < iota((heads, heads), 0))
    rank = dot(lower, by_owner) + before_in_owner
    head_ids, block_ids = iota((heads, blocks), 0), iota((heads, blocks), 1)
    pair = (block_ids % shard_blocks * heads + head_ids).astype(jnp.float32)
    slot_row = iota((128, blocks), 0)
    sums = jnp.zeros((128, blocks), jnp.float32)
    for c in range(capacity):
        hit = jnp.where((rank == c) & (needed > 0.5), pair, 0.0)
        sums = jnp.where(slot_row == 2 * c, jnp.sum(hit, axis=0, keepdims=True), sums)
        hit = jnp.where((rank == c) & (needed > 0.5), head_ids.astype(jnp.float32), 0.0)
        sums = jnp.where(slot_row == 2 * c + 1, jnp.sum(hit, axis=0, keepdims=True), sums)
    owner_t = ones(iota((seq_count, blocks), 1) // shard_blocks == iota((seq_count, blocks), 0))
    asked = lax.dot_general(
        owner_t, sums, (((1,), (1,)), ((), ())), precision=HIGHEST,
        preferred_element_type=jnp.float32,
    )
    req_ref[...] = (asked + 0.5).astype(jnp.int32)[:, None, :]
    position = (block_ids // shard_blocks * capacity).astype(jnp.float32) + rank
    lane = iota((heads, 128), 1)
    table = jnp.zeros((heads, 128), jnp.float32)
    for p in range(picks):
        here = jnp.where((before_all == p) & (needed > 0.5), position, 0.0)
        table = jnp.where(lane == p, jnp.sum(here, axis=1, keepdims=True), table)
    pos_ref[...] = (table + 0.5).astype(jnp.int32)


def order(i, me, count):
    top, next_bit = (me // (count // 2)) % 2, (me // (count // 4)) % 2
    end = (top + next_bit + 1) % 2
    return end * (1 + (i + count // 4 - 1) % (count - 1)) + (1 - end) * (count - 1 - i)


def exchange_kernel(
    seq_count, capacity, shard_blocks, picks,
    key_ref, value_ref, query_ref, perm_ref, mask_ref, got_ref, pos_ref, pos_out, query_out,
    near_key, near_value, far_key, far_value, req_ref, asked_ref, asked, send_ref, rows_ref, blocks_ref,
    load_sem, swap_send, swap_recv, req_send, req_recv, misc_sem,
    sends, recvs, relay_send, relay_recv,
):
    group, me = lax.axis_index("head"), lax.axis_index("seq")
    other = 1 - group
    near_kv, far_kv = (near_key, near_value), (far_key, far_value)
    heads, rows = near_key.shape[:2]
    barrier = pltpu.get_barrier_semaphore()
    pl.semaphore_signal(barrier, inc=1, device_id={"head": other}, device_id_type=MESH)

    def greet(step, carry):
        pl.semaphore_signal(
            barrier, inc=1, device_id={"seq": partner_of(me, step, seq_count)}, device_id_type=MESH
        )
        return carry

    lax.fori_loop(1, seq_count, greet, 0)
    loads = []
    for number, src in enumerate((key_ref, value_ref)):
        for head in range(heads):
            start_at = pl.multiple_of((group * heads + head) * HEAD_DIM, HEAD_DIM)
            loads.append(
                pltpu.make_async_copy(
                    src.at[:, pl.ds(start_at, HEAD_DIM)], near_kv[number].at[head],
                    load_sem.at[number * heads + head],
                )
            )
    for copy in loads:
        copy.start()
    pl.semaphore_wait(barrier, seq_count)

    swaps = []
    for number, src in enumerate((key_ref, value_ref)):
        for head in range(heads):
            start_at = pl.multiple_of((other * heads + head) * HEAD_DIM, HEAD_DIM)
            at = number * heads + head
            swaps.append(
                pltpu.make_async_remote_copy(
                    src_ref=src.at[:, pl.ds(start_at, HEAD_DIM)], dst_ref=far_kv[number].at[head],
                    send_sem=swap_send.at[at], recv_sem=swap_recv.at[at],
                    device_id={"head": other}, device_id_type=MESH,
                )
            )
    for copy in swaps:
        copy.start()
    route(shard_blocks, capacity, picks, mask_ref, req_ref, pos_ref)
    for b in range(shard_blocks):
        blocks_ref[b * heads : (b + 1) * heads] = perm_ref[:, b * BLOCK : (b + 1) * BLOCK][:, None, :]
    rows_ref[...] = jnp.zeros_like(rows_ref)

    def ask(step, landing):
        peer = partner_of(me, step, seq_count)
        return pltpu.make_async_remote_copy(
            src_ref=req_ref.at[peer], dst_ref=asked_ref.at[peer if landing else me],
            send_sem=req_send.at[step], recv_sem=req_recv.at[step],
            device_id={"seq": peer}, device_id_type=MESH,
        )

    def start_ask(step, carry):
        ask(step, False).start()
        return carry

    lax.fori_loop(1, seq_count, start_ask, 0)
    tell = pltpu.make_async_remote_copy(
        src_ref=pos_ref, dst_ref=pos_out, send_sem=misc_sem.at[0], recv_sem=misc_sem.at[1],
        device_id={"head": other}, device_id_type=MESH,
    )
    tell.start()
    stay = pltpu.make_async_copy(query_ref, query_out, misc_sem.at[6])
    stay.start()
    keep = pltpu.make_async_copy(req_ref.at[me], asked_ref.at[me], misc_sem.at[2])
    keep.start()
    keep.wait()

    def finish_ask(step, carry):
        ask(step, True).wait()
        return carry

    lax.fori_loop(1, seq_count, finish_ask, 0)
    to_scalar = pltpu.make_async_copy(asked_ref, asked, misc_sem.at[3])
    to_scalar.start()
    to_scalar.wait()
    base = me * (2 * rows)
    token = iota((BLOCK, rows), 1)
    near = token + (base + group * rows)
    far = token + (base + other * rows)

    def gather(which, peer):
        chosen = []
        for c in range(capacity):
            pair = jnp.clip(asked[peer, 0, 2 * c], 0, heads * shard_blocks - 1)
            rows_ref[c : c + 1, :] = blocks_ref[pair]
            chosen.append(jnp.clip(asked[peer, 0, 2 * c + 1], 0, heads - 1))
        turned = rows_ref[...].T
        for c, head in enumerate(chosen):
            column = turned[:, c : c + 1]
            near_table = (column == near).astype(jnp.float32).astype(jnp.bfloat16)
            far_table = (column == far).astype(jnp.float32).astype(jnp.bfloat16)
            got = jnp.dot(near_table, near_kv[which][head], preferred_element_type=jnp.float32)
            got += jnp.dot(far_table, far_kv[which][head], preferred_element_type=jnp.float32)
            send_ref[which, peer, c] = got.astype(jnp.bfloat16)

    def deliver(which, step, landing):
        peer = partner_of(me, step, seq_count)
        return pltpu.make_async_remote_copy(
            src_ref=send_ref.at[which, peer],
            dst_ref=got_ref.at[0, which, peer if landing else me],
            send_sem=sends.at[which, step], recv_sem=recvs.at[which, step],
            device_id={"seq": peer}, device_id_type=MESH,
        )

    def relay(which, step):
        peer = partner_of(me, step, seq_count)
        return pltpu.make_async_remote_copy(
            src_ref=got_ref.at[0, which, peer], dst_ref=got_ref.at[1, which, peer],
            send_sem=relay_send.at[which, step], recv_sem=relay_recv.at[which, step],
            device_id={"head": other}, device_id_type=MESH,
        )

    for which in range(2):
        for copy in loads[which * heads : (which + 1) * heads]:
            copy.wait()
        for copy in swaps[which * heads : (which + 1) * heads]:
            copy.wait()
        gather(which, partner_of(me, order(0, me, seq_count), seq_count))

        def produce(i, carry, which=which):
            gather(which, partner_of(me, order(i, me, seq_count), seq_count))
            deliver(which, order(i - 1, me, seq_count), False).start()
            return carry

        lax.fori_loop(1, seq_count - 1, produce, 0)
        gather(which, me)
        deliver(which, order(seq_count - 2, me, seq_count), False).start()

    locals_ = []
    for which in range(2):
        mine = pltpu.make_async_copy(
            send_ref.at[which, me], got_ref.at[0, which, me], misc_sem.at[4 + which]
        )
        share = pltpu.make_async_remote_copy(
            src_ref=send_ref.at[which, me], dst_ref=got_ref.at[1, which, me],
            send_sem=relay_send.at[which, 0], recv_sem=relay_recv.at[which, 0],
            device_id={"head": other}, device_id_type=MESH,
        )
        mine.start()
        share.start()
        locals_.extend((mine, share))

    for which in range(2):

        def pass_on(i, carry, which=which):
            step = order(i, me, seq_count)
            deliver(which, step, True).wait_recv()
            relay(which, step).start()
            return carry

        lax.fori_loop(0, seq_count - 1, pass_on, 0)

    def finish(step, carry):
        for which in range(2):
            deliver(which, step, True).wait_send()
            relay(which, step).wait()
        return carry

    lax.fori_loop(1, seq_count, finish, 0)
    for copy in locals_:
        copy.wait()
    tell.wait()
    stay.wait()


def attend_kernel(heads, picks, width, capacity, masked, pos_own, pos_far, *refs):
    if masked:
        query_ref, kv_ref, allow_ref, out_ref, stage, sems = refs
    else:
        query_ref, kv_ref, out_ref, stage, sems = refs
    group = lax.axis_index("head")
    scale = math.log2(math.e) / math.sqrt(HEAD_DIM)
    ones = jnp.ones((BLOCK, HEAD_DIM), jnp.bfloat16)
    span = width * HEAD_DIM
    batches = query_ref.shape[1] // span

    def put(batch, buffer):
        return pltpu.make_async_copy(
            stage.at[buffer],
            out_ref.at[:, pl.ds(pl.multiple_of(batch * span, span), span)],
            sems.at[buffer],
        )

    def one(batch, carry):
        where_, scores = [], []
        for w in range(width):
            head = batch * width + w
            away = (head // heads) != group
            local = head % heads
            query = query_ref[:, pl.ds(pl.multiple_of(head * HEAD_DIM, HEAD_DIM), HEAD_DIM)]
            for p in range(picks):
                slot = jnp.where(away, pos_far[local, p], pos_own[local, p])
                spot = (slot // capacity, slot % capacity)
                rel = away.astype(jnp.int32)
                where_.append((rel, spot))
                score = lax.dot_general(
                    query, kv_ref[rel, 0, spot[0], spot[1]], (((1,), (1,)), ((), ())),
                    preferred_element_type=jnp.float32,
                )
                if masked:
                    score = jnp.where(allow_ref[head, :, p : p + 1] > 0, score, -jnp.inf)
                scores.append(score)
        weights = []
        for w in range(width):
            own = scores[w * picks : (w + 1) * picks]
            top = jnp.max(functools.reduce(jnp.maximum, own), axis=1, keepdims=True)
            weights.extend([jnp.exp2((s - top) * scale).astype(jnp.bfloat16) for s in own])
        buffer = batch % 2

        @pl.when(batch >= 2)
        def _():
            put(batch - 2, buffer).wait()

        for w in range(width):
            parts = []
            for p in range(picks):
                rel, spot = where_[w * picks + p]
                parts.append(
                    jnp.dot(
                        weights[w * picks + p],
                        jnp.concatenate([kv_ref[rel, 1, spot[0], spot[1]], ones], axis=1),
                        preferred_element_type=jnp.float32,
                    )
                )
            mixed = functools.reduce(jnp.add, parts)
            stage[buffer, :, w * HEAD_DIM : (w + 1) * HEAD_DIM] = (
                mixed[:, :HEAD_DIM] / mixed[:, HEAD_DIM:]
            ).astype(jnp.bfloat16)
        put(batch, buffer).start()
        return carry

    lax.fori_loop(0, batches, one, 0)
    for batch in range(max(0, batches - 2), batches):
        put(batch, batch % 2).wait()


def token_allow(cluster_perm, block_mask, picks, me, shard_rows):
    needed = jnp.max(block_mask, axis=1)
    prefix = jnp.cumsum(needed, axis=1) - needed
    chosen = (needed[:, :, None] == 1) & (prefix[:, :, None] == jnp.arange(picks)[None, None, :])
    live = jnp.einsum(
        "hqb,hbp->hqp", block_mask.astype(jnp.float32), chosen.astype(jnp.float32)
    )
    group_heads = cluster_perm.shape[0]
    local = cluster_perm - me * shard_rows
    place = jnp.zeros((group_heads, shard_rows), jnp.int32)
    place = place.at[jnp.arange(group_heads)[:, None], local].set(
        jnp.broadcast_to(jnp.arange(shard_rows, dtype=jnp.int32) // BLOCK, local.shape)
    )
    by_token = jnp.take_along_axis(live, place[:, :, None], axis=1).astype(jnp.float32)
    return lax.all_to_all(by_token, "head", split_axis=1, concat_axis=0, tiled=True)


def shards(queries, key_states, value_states, cluster_perm, block_mask):
    group_heads, shard_rows = cluster_perm.shape
    shard_blocks = shard_rows // BLOCK
    seq_count = lax.axis_size("seq")
    block_total = block_mask.shape[2]
    picks = max(1, block_total // 64)
    capacity = max(
        1, min(shard_blocks, (group_heads * picks * 8 + 5 * seq_count - 1) // (5 * seq_count))
    )
    rows, columns = queries.shape
    me = lax.axis_index("seq")
    vmem = pl.BlockSpec(memory_space=pltpu.VMEM)
    anywhere = pl.BlockSpec(memory_space=pltpu.HBM)
    struct = jax.ShapeDtypeStruct
    bf16, i32 = jnp.bfloat16, jnp.int32

    dma = pltpu.SemaphoreType.DMA
    kv_half = pltpu.VMEM((group_heads, rows, HEAD_DIM), bf16)
    table = struct((group_heads, 128), i32)
    resident = 2 * (4 * seq_count * capacity * BLOCK * HEAD_DIM + rows * columns)
    grant = 67043328 - resident - 256 * 1024
    got, positions, pos_far, near_queries = pl.pallas_call(
        functools.partial(exchange_kernel, seq_count, capacity, shard_blocks, picks),
        out_shape=(
            pltpu.VMEM((2, 2, seq_count, capacity, BLOCK, HEAD_DIM), bf16), table, table,
            pltpu.VMEM((rows, columns), bf16),
        ),
        in_specs=[anywhere, anywhere, anywhere, vmem, vmem],
        out_specs=(vmem, vmem, vmem, vmem),
        scratch_shapes=[
            kv_half, kv_half, kv_half, kv_half,
            pltpu.VMEM((seq_count, 1, 128), i32),
            pltpu.VMEM((seq_count, 1, 128), i32),
            pltpu.SMEM((seq_count, 1, 128), i32),
            pltpu.VMEM((2, seq_count, capacity, BLOCK, HEAD_DIM), bf16),
            pltpu.VMEM((8 * -(-capacity // 8), 128), i32),
            pltpu.VMEM((shard_blocks * group_heads, 1, BLOCK), i32),
            dma((2 * group_heads,)), dma((2 * group_heads,)), dma((2 * group_heads,)),
            dma((seq_count,)), dma((seq_count,)), dma((7,)),
        ] + [dma((2, seq_count)) for _ in range(4)],
        compiler_params=pltpu.CompilerParams(
            collective_id=0, has_side_effects=True, vmem_limit_bytes=grant
        ),
        name="exchange",
    )(key_states, value_states, queries, cluster_perm, block_mask)

    masked = picks > 1
    total_heads = columns // HEAD_DIM
    width = 8 if total_heads % 8 == 0 else 1
    operands = [near_queries, got]
    if masked:
        operands.append(token_allow(cluster_perm, block_mask, picks, me, shard_rows))
    smem = pl.BlockSpec(memory_space=pltpu.SMEM)
    return pl.pallas_call(
        functools.partial(attend_kernel, group_heads, picks, width, capacity, masked),
        out_shape=struct((rows, columns), bf16),
        in_specs=[smem, smem] + [vmem] * len(operands),
        out_specs=anywhere,
        scratch_shapes=[pltpu.VMEM((2, rows, width * HEAD_DIM), bf16), dma((2,))],
        compiler_params=pltpu.CompilerParams(vmem_limit_bytes=24 * 1024 * 1024),
        name="attend",
    )(positions, pos_far, *operands)


def solution(mesh):
    rows = P(("seq", "head"), None)
    placed = (rows, rows, rows, P("head", "seq"), P("head", "seq", None))
    return jax.shard_map(shards, mesh=mesh, in_specs=placed, out_specs=rows, check_vma=False)
```

profile of v0, /device:TPU:1, one launch (start us, length us, event | category | flops | bytes accessed | tf_op | source)
XLA Modules:
  0.0 72.7 jit_solution(1667260382164172901)
XLA Ops:
  0.0 64.6 %exchange.1 = (bf16[2,2,16,2,128,128]{5,4,3,2,1,0:T(8,128)(2,1)S(1)}, s32[20,128]{1,0:T(8,128)}, s32[20,128]{1,0:T(8,128)}, bf16[256,5120]{1,0:T(8,128)(2,1)S(1)}) custom-call(bf16[256,5120]{1,0:T(8,128)(2,1)} %key_ref.1, bf16[256,5120]{1,0:T(8,128)(2,1)} %value_ref.1, bf16[256,5120]{1,0:T(8,128)(2,1)} %query_ref.1, s32[20,512]{1,0:T(8,128)} %perm_ref.1, ...), custom_call_target="tpu_custom_call" | custom-call | tf_op jit(solution)/shard_map/exchange/pallas_call | solution.py:360
  64.6 0.0 copy-start
  64.6 0.7 copy-done
  65.3 0.0 copy-start.1
  65.3 0.7 copy-done.1
  66.0 6.6 %attend.1 = bf16[256,5120]{1,0:T(8,128)(2,1)} custom-call(s32[20,128]{1,0:T(8,128)S(1)} %copy-done, s32[20,128]{1,0:T(8,128)S(1)} %copy-done.1, bf16[256,5120]{1,0:T(8,128)(2,1)S(1)} %get-tuple-element.11.refs_0_, bf16[2,2,16,2,128,128]{5,4,3,2,1,0:T(8,128)(2,1)S(1)} %get-tuple-element.12.refs_1_), custom_call_target="tpu_custom_call" | custom-call | tf_op jit(solution)/shard_map/attend/pallas_call | solution.py:392
Async XLA Ops:
  64.6 0.7 copy-start
  65.3 0.7 copy-start.1
where the time goes:
time: 73.1 us; the launch traced here: 72.7 us
  Pallas kernels  71.2 us (97%)
  local copies, waits for them, and re-layouts  1.41 us (2%)
    pallas_call x1, Pallas kernels, shards(): pl.pallas_call(functools.partial(exchange_kernel, seq_count, capacity, sh...  64.6 us
    pallas_call x1, Pallas kernels, shards(): pl.pallas_call(functools.partial(attend_kernel, group_heads, picks, width...  6.65 us

commit v1 on v0

--- a/solution.py
+++ b/solution.py
@@ -248,6 +248,356 @@
     stay.wait()
 
 
+def fused_kernel(
+    seq_count, capacity, shard_blocks, picks,
+    key_ref, value_ref, query_hbm, perm_ref, mask_ref, out_ref,
+    keys, values, query_ref, send_ref, got_ref, stage_ref,
+    req_ref, far_req_ref, asked_ref, pos_ref, far_pos_ref, rows_ref, blocks_ref,
+    own_tab, far_tab, asked_near, asked, own_pos, far_pos,
+    load_sem, swap_send, swap_recv, req_send, req_recv, misc_sem, tab_sem,
+    near_sends, near_recvs, sends, recvs, relay_send, relay_recv, step_sem,
+):
+    group, me = lax.axis_index("head"), lax.axis_index("seq")
+    other = 1 - group
+    heads = perm_ref.shape[0]
+    rows, columns = out_ref.shape
+    half = heads * HEAD_DIM
+    peer_of = lambda step: partner_of(me, step, seq_count)
+    top, low = (me // 8) % 2, (me // 4) % 2
+    edge = (top + low + 1) % 2
+
+    def near_step(i):
+        far = (3 - i) // 2
+        return 8 * far + 4 * (edge * ((i + 1) % 2) + (1 - edge) * ((i + 1) // 2))
+
+    def rest_step(i):
+        q = i // 3
+        first, second = (3 - q) // 2, ((q + 1) // 2) % 2
+        plane = edge * (4 * first + 8 * second) + (1 - edge) * (8 * first + 4 * second)
+        return plane + 1 + i % 3
+
+    def times(count, body):
+        lax.fori_loop(0, count, lambda i, carry: (body(i), carry)[1], 0)
+
+    barrier = pltpu.get_barrier_semaphore()
+    pl.semaphore_signal(barrier, inc=1, device_id={"head": other}, device_id_type=MESH)
+    for step in (4, 8, 12, 1, 2):
+        pl.semaphore_signal(barrier, inc=1, device_id={"seq": peer_of(step)}, device_id_type=MESH)
+
+    loads, swaps = [], []
+    parts = load_sem.shape[1]
+    span = half // parts
+    here = pl.ds(pl.multiple_of(group * rows, rows), rows)
+    for number, (src, dst) in enumerate(((key_ref, keys), (value_ref, values))):
+        for part in range(parts):
+            at = pl.ds(part * span, span)
+            mine = pl.ds(pl.multiple_of(group * half + part * span, HEAD_DIM), span)
+            theirs = pl.ds(pl.multiple_of(other * half + part * span, HEAD_DIM), span)
+            loads.append(
+                pltpu.make_async_copy(
+                    src.at[:, mine], dst.at[here, at], load_sem.at[number, part]
+                )
+            )
+            swaps.append(
+                pltpu.make_async_remote_copy(
+                    src_ref=src.at[:, theirs], dst_ref=dst.at[here, at],
+                    send_sem=swap_send.at[number, part], recv_sem=swap_recv.at[number, part],
+                    device_id={"head": other}, device_id_type=MESH,
+                )
+            )
+    for copy in loads:
+        copy.start()
+    take = pltpu.make_async_copy(query_hbm, query_ref, misc_sem.at[0])
+    take.start()
+    route(shard_blocks, capacity, picks, mask_ref, req_ref, pos_ref)
+    for b in range(shard_blocks):
+        blocks_ref[b * heads : (b + 1) * heads] = perm_ref[:, b * BLOCK : (b + 1) * BLOCK][:, None, :]
+    rows_ref[...] = jnp.zeros_like(rows_ref)
+    pl.semaphore_wait(barrier, 6)
+
+    def ask(step, landing):
+        peer = peer_of(step)
+        return pltpu.make_async_remote_copy(
+            src_ref=req_ref.at[peer], dst_ref=asked_ref.at[peer if landing else me],
+            send_sem=req_send.at[step], recv_sem=req_recv.at[step],
+            device_id={"seq": peer}, device_id_type=MESH,
+        )
+
+    times(3, lambda i: ask(near_step(i), False).start())
+    for copy in swaps:
+        copy.start()
+    for number, step in enumerate((1, 2)):
+        pl.semaphore_signal(
+            step_sem.at[number], inc=1, device_id={"seq": peer_of(step)}, device_id_type=MESH
+        )
+    tells = []
+    for number, (src, dst) in enumerate(((req_ref, far_req_ref), (pos_ref, far_pos_ref))):
+        tells.append(
+            pltpu.make_async_remote_copy(
+                src_ref=src, dst_ref=dst,
+                send_sem=misc_sem.at[1 + number], recv_sem=misc_sem.at[3 + number],
+                device_id={"head": other}, device_id_type=MESH,
+            )
+        )
+    for copy in tells:
+        copy.start()
+    keep = pltpu.make_async_copy(req_ref.at[me], asked_ref.at[me], misc_sem.at[5])
+    keep.start()
+    own_tabs = [
+        pltpu.make_async_copy(req_ref, own_tab, tab_sem.at[0]),
+        pltpu.make_async_copy(pos_ref, own_pos, tab_sem.at[1]),
+    ]
+    for copy in own_tabs:
+        copy.start()
+    pl.semaphore_wait(step_sem.at[0], 1)
+    pl.semaphore_wait(step_sem.at[1], 1)
+    pl.semaphore_signal(step_sem.at[2], inc=1, device_id={"seq": peer_of(2)}, device_id_type=MESH)
+    pl.semaphore_wait(step_sem.at[2], 1)
+    times(12, lambda i: ask(rest_step(i), False).start())
+
+    def near_scalar(i):
+        peer = peer_of(4 * i + 4)
+        return pltpu.make_async_copy(asked_ref.at[peer], asked_near.at[peer], tab_sem.at[5 + i])
+
+    for i in range(3):
+        ask(4 * i + 4, True).wait_recv()
+        near_scalar(i).start()
+    for i in range(3):
+        near_scalar(i).wait()
+
+    token = iota((BLOCK, 2 * rows), 1) + me * (2 * rows)
+    sides = (keys, values)
+
+    def gather(table_ref, peer, whiches, put):
+        chosen = []
+        for c in range(capacity):
+            pair = jnp.clip(table_ref[peer, 0, 2 * c], 0, heads * shard_blocks - 1)
+            rows_ref[c : c + 1, :] = blocks_ref[pair]
+            head = jnp.clip(table_ref[peer, 0, 2 * c + 1], 0, heads - 1)
+            chosen.append(head * HEAD_DIM)
+        turned = rows_ref[...].T
+        for c, start_at in enumerate(chosen):
+            table = (turned[:, c : c + 1] == token).astype(jnp.float32).astype(jnp.bfloat16)
+            for which in whiches:
+                got = jnp.dot(
+                    table, sides[which][:, pl.ds(start_at, HEAD_DIM)],
+                    preferred_element_type=jnp.float32,
+                )
+                put(which, c, got.astype(jnp.bfloat16))
+
+    def to_send(peer):
+        def put(which, c, got):
+            send_ref[peer, which, c] = got
+
+        return put
+
+    def near_deliver(which, step, landing):
+        peer = peer_of(step)
+        return pltpu.make_async_remote_copy(
+            src_ref=send_ref.at[peer, which], dst_ref=got_ref.at[0, peer if landing else me, which],
+            send_sem=near_sends.at[which, step], recv_sem=near_recvs.at[which, step],
+            device_id={"seq": peer}, device_id_type=MESH,
+        )
+
+    def deliver(step, landing):
+        peer = peer_of(step)
+        return pltpu.make_async_remote_copy(
+            src_ref=send_ref.at[peer], dst_ref=got_ref.at[0, peer if landing else me],
+            send_sem=sends.at[step], recv_sem=recvs.at[step],
+            device_id={"seq": peer}, device_id_type=MESH,
+        )
+
+    def relay(step, landing):
+        peer = peer_of(step)
+        return pltpu.make_async_remote_copy(
+            src_ref=got_ref.at[0, peer], dst_ref=got_ref.at[1, peer],
+            send_sem=relay_send.at[step], recv_sem=relay_recv.at[step],
+            device_id={"head": other}, device_id_type=MESH,
+        )
+
+    for which in range(2):
+        for copy in loads[which * parts : (which + 1) * parts]:
+            copy.wait()
+        for copy in swaps[which * parts : (which + 1) * parts]:
+            copy.wait()
+
+        def serve(i, which=which):
+            step = near_step(i)
+            peer = peer_of(step)
+            gather(asked_near, peer, (which,), to_send(peer))
+            near_deliver(which, step, False).start()
+
+        times(3, serve)
+    for copy in own_tabs:
+        copy.wait()
+
+    keep.wait()
+    times(12, lambda i: ask(rest_step(i), True).wait_recv())
+    to_scalar = pltpu.make_async_copy(asked_ref, asked, tab_sem.at[4])
+    to_scalar.start()
+    to_scalar.wait()
+
+    def produce(i):
+        step = rest_step(i)
+        peer = peer_of(step)
+        gather(asked, peer, (0, 1), to_send(peer))
+        deliver(step, False).start()
+
+    times(12, produce)
+
+    def to_got(which, c, got):
+        got_ref[0, me, which, c] = got
+
+    gather(own_tab, me, (0, 1), to_got)
+    relay(0, False).start()
+    for copy in tells:
+        copy.wait()
+    far_tabs = [
+        pltpu.make_async_copy(far_req_ref, far_tab, tab_sem.at[2]),
+        pltpu.make_async_copy(far_pos_ref, far_pos, tab_sem.at[3]),
+    ]
+    for copy in far_tabs:
+        copy.start()
+    for copy in far_tabs:
+        copy.wait()
+    take.wait()
+
+    scale = math.log2(math.e) / math.sqrt(HEAD_DIM)
+    ones = jnp.ones((BLOCK, HEAD_DIM), jnp.bfloat16)
+
+    def attend(items):
+        scores = []
+        for rel, peer, c in items:
+            tab, base = ((own_tab, group), (far_tab, other))[rel]
+            head = base * heads + jnp.clip(tab[peer, 0, 2 * c + 1], 0, heads - 1)
+            query = query_ref[:, pl.ds(head * HEAD_DIM, HEAD_DIM)]
+            scores.append(
+                lax.dot_general(
+                    query, got_ref[rel, peer, 0, c], (((1,), (1,)), ((), ())),
+                    preferred_element_type=jnp.float32,
+                )
+            )
+        weights = []
+        for score in scores:
+            peak = jnp.max(score, axis=1, keepdims=True)
+            weights.append(jnp.exp2((score - peak) * scale).astype(jnp.bfloat16))
+        for (rel, peer, c), weight in zip(items, weights):
+            mixed = jnp.dot(
+                weight, jnp.concatenate([got_ref[rel, peer, 1, c], ones], axis=1),
+                preferred_element_type=jnp.float32,
+            )
+            stage_ref[rel, peer * capacity + c] = (mixed[:, :HEAD_DIM] / mixed[:, HEAD_DIM:]).astype(jnp.bfloat16)
+
+    slots = lambda rel, peer: [(rel, peer, c) for c in range(capacity)]
+    attend(slots(0, me))
+    relay(0, True).wait_recv()
+    attend(slots(1, me))
+
+    def near_take(i):
+        step = near_step(i)
+        for which in range(2):
+            near_deliver(which, step, True).wait_recv()
+        relay(step, False).start()
+
+    times(3, near_take)
+
+    def near_use(i):
+        step = near_step(i)
+        peer = peer_of(step)
+        relay(step, True).wait_recv()
+        attend(slots(0, peer) + slots(1, peer))
+
+    times(3, near_use)
+
+    def use(step, before):
+        deliver(step, True).wait_recv()
+        relay(step, False).start()
+        if before is None:
+            attend(slots(0, peer_of(step)))
+        else:
+            relay(before, True).wait_recv()
+            attend(slots(0, peer_of(step)) + slots(1, peer_of(before)))
+
+    close = lambda j: 1 + j + j // 3
+    away = lambda k: 9 + k // 2 + 4 * (k % 2)
+    use(close(0), None)
+    times(5, lambda j: use(close(j + 1), close(j)))
+    use(away(0), close(5))
+    times(5, lambda k: use(away(k + 1), away(k)))
+    relay(away(5), True).wait_recv()
+    attend(slots(1, peer_of(away(5))))
+
+    for rel, (tab, base) in enumerate(((own_pos, group), (far_pos, other))):
+
+        def place(local, rel=rel, tab=tab, base=base):
+            slot = jnp.clip(tab[local, 0], 0, seq_count * capacity - 1)
+            at = pl.multiple_of((base * heads + local) * HEAD_DIM, HEAD_DIM)
+            out_ref[:, pl.ds(at, HEAD_DIM)] = stage_ref[rel, slot]
+
+        times(heads, place)
+
+    def finish_near(i):
+        step = near_step(i)
+        ask(step, True).wait_send()
+        for which in range(2):
+            near_deliver(which, step, True).wait_send()
+        relay(step, True).wait_send()
+
+    times(3, finish_near)
+
+    def finish(i):
+        step = rest_step(i)
+        ask(step, True).wait_send()
+        deliver(step, True).wait_send()
+        relay(step, True).wait_send()
+
+    times(12, finish)
+    relay(0, True).wait_send()
+
+
+def fused(key_states, value_states, queries, cluster_perm, block_mask, capacity, picks):
+    heads, shard_rows = cluster_perm.shape
+    shard_blocks = shard_rows // BLOCK
+    seq_count = lax.axis_size("seq")
+    rows, columns = queries.shape
+    vmem = pl.BlockSpec(memory_space=pltpu.VMEM)
+    anywhere = pl.BlockSpec(memory_space=pltpu.HBM)
+    bf16, i32 = jnp.bfloat16, jnp.int32
+    dma = pltpu.SemaphoreType.DMA
+    table = (seq_count, 1, 128)
+    parts = 4
+    return pl.pallas_call(
+        functools.partial(fused_kernel, seq_count, capacity, shard_blocks, picks),
+        out_shape=pltpu.VMEM((rows, columns), bf16),
+        in_specs=[anywhere, anywhere, anywhere, vmem, vmem],
+        out_specs=vmem,
+        scratch_shapes=[
+            pltpu.VMEM((shard_rows, heads * HEAD_DIM), bf16),
+            pltpu.VMEM((shard_rows, heads * HEAD_DIM), bf16),
+            pltpu.VMEM((rows, columns), bf16),
+            pltpu.VMEM((seq_count, 2, capacity, BLOCK, HEAD_DIM), bf16),
+            pltpu.VMEM((2, seq_count, 2, capacity, BLOCK, HEAD_DIM), bf16),
+            pltpu.VMEM((2, seq_count * capacity, rows, HEAD_DIM), bf16),
+            pltpu.VMEM(table, i32), pltpu.VMEM(table, i32), pltpu.VMEM(table, i32),
+            pltpu.VMEM((heads, 128), i32), pltpu.VMEM((heads, 128), i32),
+            pltpu.VMEM((8 * -(-capacity // 8), 128), i32),
+            pltpu.VMEM((shard_blocks * heads, 1, BLOCK), i32),
+            pltpu.SMEM(table, i32), pltpu.SMEM(table, i32), pltpu.SMEM(table, i32),
+            pltpu.SMEM(table, i32),
+            pltpu.SMEM((heads, 128), i32), pltpu.SMEM((heads, 128), i32),
+            dma((2, parts)), dma((2, parts)), dma((2, parts)),
+            dma((seq_count,)), dma((seq_count,)), dma((6,)), dma((8,)),
+            dma((2, seq_count)), dma((2, seq_count)),
+            dma((seq_count,)), dma((seq_count,)), dma((seq_count,)), dma((seq_count,)),
+            pltpu.SemaphoreType.REGULAR((3,)),
+        ],
+        compiler_params=pltpu.CompilerParams(
+            collective_id=1, has_side_effects=True, vmem_limit_bytes=40 * 1024 * 1024
+        ),
+        name="fused",
+    )(key_states, value_states, queries, cluster_perm, block_mask)
+
+
 def attend_kernel(heads, picks, width, capacity, masked, pos_own, pos_far, *refs):
     if masked:
         query_ref, kv_ref, allow_ref, out_ref, stage, sems = refs
@@ -347,6 +697,10 @@
     )
     rows, columns = queries.shape
     me = lax.axis_index("seq")
+    if picks == 1 and seq_count == 16:
+        return fused(
+            key_states, value_states, queries, cluster_perm, block_mask, capacity, picks
+        )
     vmem = pl.BlockSpec(memory_space=pltpu.VMEM)
     anywhere = pl.BlockSpec(memory_space=pltpu.HBM)
     struct = jax.ShapeDtypeStruct

time: 73.1 us -> 68.1 us (0.932)
  the two profiles are of different devices: /device:TPU:1 before, /device:TPU:9 now
where the time goes in v1:
time: 68.1 us; the launch traced here: 67.8 us
  Pallas kernels  59.5 us (87%)
  local copies, waits for them, and re-layouts  8.29 us (12%)
    pallas_call x1, Pallas kernels, fused(): pl.pallas_call(functools.partial(fused_kernel, seq_count, capacity, shard...  59.5 us
    unnamed x11, local copies, waits for them, and re-layouts  8.29 us

profile of v1, /device:TPU:9, one launch (start us, length us, event | category | flops | bytes accessed | tf_op | source)
XLA Modules:
  0.0 67.8 jit_solution(6957043911805010983)
XLA Ops:
  0.0 0.0 copy-start
  0.0 1.7 %copy-done = bf16[256,5120]{1,0:T(8,128)(2,1)S(1)} copy-done((bf16[256,5120]{1,0:T(8,128)(2,1)S(1)}, bf16[256,5120]{1,0:T(8,128)(2,1)}, u32[]{:S(2)}) %copy-start) | copy-done | bytes 2621464
  1.7 0.0 copy-start.1
  1.7 1.7 %copy-done.1 = bf16[256,5120]{1,0:T(8,128)(2,1)S(1)} copy-done((bf16[256,5120]{1,0:T(8,128)(2,1)S(1)}, bf16[256,5120]{1,0:T(8,128)(2,1)}, u32[]{:S(2)}) %copy-start.1) | copy-done | bytes 2621464
  3.5 0.0 copy-start.2
  3.5 1.7 %copy-done.2 = bf16[256,5120]{1,0:T(8,128)(2,1)S(1)} copy-done((bf16[256,5120]{1,0:T(8,128)(2,1)S(1)}, bf16[256,5120]{1,0:T(8,128)(2,1)}, u32[]{:S(2)}) %copy-start.2) | copy-done | bytes 2621464
  5.2 0.0 copy-start.3
  5.2 0.8 %copy-done.3 = s32[20,512]{1,0:T(8,128)S(1)} copy-done((s32[20,512]{1,0:T(8,128)S(1)}, s32[20,512]{1,0:T(8,128)}, u32[]{:S(2)}) %copy-start.3) | copy-done | bytes 40984
  6.0 0.0 copy-start.4
  6.0 0.8 %copy-done.4 = s32[20,4,64]{2,1,0:T(4,128)S(1)} copy-done((s32[20,4,64]{2,1,0:T(4,128)S(1)}, s32[20,4,64]{2,1,0:T(4,128)}, u32[]{:S(2)}) %copy-start.4) | copy-done | bytes 20504
  6.8 59.5 %fused.1 = bf16[256,5120]{1,0:T(8,128)(2,1)S(1)} custom-call(bf16[256,5120]{1,0:T(8,128)(2,1)S(1)} %copy-done, bf16[256,5120]{1,0:T(8,128)(2,1)S(1)} %copy-done.1, bf16[256,5120]{1,0:T(8,128)(2,1)S(1)} %copy-done.2, s32[20,512]{1,0:T(8,128)S(1)} %copy-done.3, s32[20,4,64]{2,1,0:T(4,128)S(1)} %copy-done.4), custom_call_target="tpu_custom_call" | custom-call | tf_op jit(solution)/shard_map/fused/pallas_call | solution.py:569
  66.3 1.5 %copy.7 = bf16[256,5120]{1,0:T(8,128)(2,1)} copy(bf16[256,5120]{1,0:T(8,128)(2,1)S(1)} %fused.1) | data formatting | bytes 5242880
Async XLA Ops:
  0.0 1.7 %copy-start = (bf16[256,5120]{1,0:T(8,128)(2,1)S(1)}, bf16[256,5120]{1,0:T(8,128)(2,1)}, u32[]{:S(2)}) copy-start(bf16[256,5120]{1,0:T(8,128)(2,1)} %key_ref.1) | copy-start | bytes 7864324
  1.7 1.7 %copy-start.1 = (bf16[256,5120]{1,0:T(8,128)(2,1)S(1)}, bf16[256,5120]{1,0:T(8,128)(2,1)}, u32[]{:S(2)}) copy-start(bf16[256,5120]{1,0:T(8,128)(2,1)} %value_ref.1) | copy-start | bytes 7864324
  3.5 1.7 %copy-start.2 = (bf16[256,5120]{1,0:T(8,128)(2,1)S(1)}, bf16[256,5120]{1,0:T(8,128)(2,1)}, u32[]{:S(2)}) copy-start(bf16[256,5120]{1,0:T(8,128)(2,1)} %query_hbm.1) | copy-start | bytes 7864324
  5.2 0.8 %copy-start.3 = (s32[20,512]{1,0:T(8,128)S(1)}, s32[20,512]{1,0:T(8,128)}, u32[]{:S(2)}) copy-start(s32[20,512]{1,0:T(8,128)} %perm_ref.1) | copy-start | bytes 122884
  6.0 0.8 %copy-start.4 = (s32[20,4,64]{2,1,0:T(4,128)S(1)}, s32[20,4,64]{2,1,0:T(4,128)}, u32[]{:S(2)}) copy-start(s32[20,4,64]{2,1,0:T(4,128)} %mask_ref.1) | copy-start | bytes 61444

commit v2 on v1

--- a/solution.py
+++ b/solution.py
@@ -250,8 +250,8 @@
 
 def fused_kernel(
     seq_count, capacity, shard_blocks, picks,
-    key_ref, value_ref, query_hbm, perm_ref, mask_ref, out_ref,
-    keys, values, query_ref, send_ref, got_ref, stage_ref,
+    key_ref, value_ref, query_hbm, perm_hbm, mask_hbm, out_ref,
+    perm_ref, mask_ref, keys, values, query_ref, send_ref, got_ref, stage_ref,
     req_ref, far_req_ref, asked_ref, pos_ref, far_pos_ref, rows_ref, blocks_ref,
     own_tab, far_tab, asked_near, asked, own_pos, far_pos,
     load_sem, swap_send, swap_recv, req_send, req_recv, misc_sem, tab_sem,
@@ -270,11 +270,13 @@
         far = (3 - i) // 2
         return 8 * far + 4 * (edge * ((i + 1) % 2) + (1 - edge) * ((i + 1) // 2))
 
-    def rest_step(i):
-        q = i // 3
-        first, second = (3 - q) // 2, ((q + 1) // 2) % 2
-        plane = edge * (4 * first + 8 * second) + (1 - edge) * (8 * first + 4 * second)
-        return plane + 1 + i % 3
+    def far_step(k):
+        return 9 + k // 2 + 4 * (edge * ((k + 1) % 2) + (1 - edge) * (k % 2))
+
+    def all_rest(body):
+        times(3, lambda k: body(1 + k))
+        times(3, lambda k: body(5 + k))
+        times(6, lambda k: body(far_step(k)))
 
     def times(count, body):
         lax.fori_loop(0, count, lambda i, carry: (body(i), carry)[1], 0)
@@ -284,6 +286,10 @@
     for step in (4, 8, 12, 1, 2):
         pl.semaphore_signal(barrier, inc=1, device_id={"seq": peer_of(step)}, device_id_type=MESH)
 
+    masks = pltpu.make_async_copy(mask_hbm, mask_ref, misc_sem.at[6])
+    masks.start()
+    perms = pltpu.make_async_copy(perm_hbm, perm_ref, misc_sem.at[7])
+    perms.start()
     loads, swaps = [], []
     parts = load_sem.shape[1]
     span = half // parts
@@ -309,7 +315,9 @@
         copy.start()
     take = pltpu.make_async_copy(query_hbm, query_ref, misc_sem.at[0])
     take.start()
+    masks.wait()
     route(shard_blocks, capacity, picks, mask_ref, req_ref, pos_ref)
+    perms.wait()
     for b in range(shard_blocks):
         blocks_ref[b * heads : (b + 1) * heads] = perm_ref[:, b * BLOCK : (b + 1) * BLOCK][:, None, :]
     rows_ref[...] = jnp.zeros_like(rows_ref)
@@ -353,7 +361,7 @@
     pl.semaphore_wait(step_sem.at[1], 1)
     pl.semaphore_signal(step_sem.at[2], inc=1, device_id={"seq": peer_of(2)}, device_id_type=MESH)
     pl.semaphore_wait(step_sem.at[2], 1)
-    times(12, lambda i: ask(rest_step(i), False).start())
+    all_rest(lambda step: ask(step, False).start())
 
     def near_scalar(i):
         peer = peer_of(4 * i + 4)
@@ -432,18 +440,23 @@
         copy.wait()
 
     keep.wait()
-    times(12, lambda i: ask(rest_step(i), True).wait_recv())
+    all_rest(lambda step: ask(step, True).wait_recv())
     to_scalar = pltpu.make_async_copy(asked_ref, asked, tab_sem.at[4])
     to_scalar.start()
     to_scalar.wait()
 
-    def produce(i):
-        step = rest_step(i)
+    def produce(step):
         peer = peer_of(step)
         gather(asked, peer, (0, 1), to_send(peer))
         deliver(step, False).start()
 
-    times(12, produce)
+    def produce_at(i):
+        far = edge * ((i + 6) // 9) + (1 - edge) * ((14 - i) // 9)
+        at = i - 3 * edge + 9 * (1 - far)
+        produce(far * far_step(at % 9) + (1 - far) * (5 + (at + 9 * edge) % 3))
+
+    times(9, produce_at)
+    times(3, lambda k: produce(1 + k))
 
     def to_got(which, c, got):
         got_ref[0, me, which, c] = got
@@ -545,13 +558,12 @@
 
     times(3, finish_near)
 
-    def finish(i):
-        step = rest_step(i)
+    def finish(step):
         ask(step, True).wait_send()
         deliver(step, True).wait_send()
         relay(step, True).wait_send()
 
-    times(12, finish)
+    all_rest(finish)
     relay(0, True).wait_send()
 
 
@@ -569,9 +581,10 @@
     return pl.pallas_call(
         functools.partial(fused_kernel, seq_count, capacity, shard_blocks, picks),
         out_shape=pltpu.VMEM((rows, columns), bf16),
-        in_specs=[anywhere, anywhere, anywhere, vmem, vmem],
+        in_specs=[anywhere] * 5,
         out_specs=vmem,
         scratch_shapes=[
+            pltpu.VMEM(cluster_perm.shape, i32), pltpu.VMEM(block_mask.shape, i32),
             pltpu.VMEM((shard_rows, heads * HEAD_DIM), bf16),
             pltpu.VMEM((shard_rows, heads * HEAD_DIM), bf16),
             pltpu.VMEM((rows, columns), bf16),
@@ -586,13 +599,13 @@
             pltpu.SMEM(table, i32),
             pltpu.SMEM((heads, 128), i32), pltpu.SMEM((heads, 128), i32),
             dma((2, parts)), dma((2, parts)), dma((2, parts)),
-            dma((seq_count,)), dma((seq_count,)), dma((6,)), dma((8,)),
+            dma((seq_count,)), dma((seq_count,)), dma((8,)), dma((8,)),
             dma((2, seq_count)), dma((2, seq_count)),
             dma((seq_count,)), dma((seq_count,)), dma((seq_count,)), dma((seq_count,)),
             pltpu.SemaphoreType.REGULAR((3,)),
         ],
         compiler_params=pltpu.CompilerParams(
-            collective_id=1, has_side_effects=True, vmem_limit_bytes=40 * 1024 * 1024
+            collective_id=1, has_side_effects=True, vmem_limit_bytes=67043328 - 2 * rows * columns - 256 * 1024
         ),
         name="fused",
     )(key_states, value_states, queries, cluster_perm, block_mask)

time: 68.1 us -> 62.1 us (0.912)
  the two profiles are of different devices: /device:TPU:9 before, /device:TPU:1 now
where the time goes in v2:
time: 62.1 us; the launch traced here: 62 us
  Pallas kernels  60.5 us (97%)
  local copies, waits for them, and re-layouts  1.49 us (2%)
    pallas_call x1, Pallas kernels, fused(): pl.pallas_call(functools.partial(fused_kernel, seq_count, capacity, shard...  60.5 us
    unnamed x1, local copies, waits for them, and re-layouts  1.49 us

profile of v2, /device:TPU:1, one launch (start us, length us, event | category | flops | bytes accessed | tf_op | source)
XLA Modules:
  0.0 62.0 jit_solution(5762262245940137287)
XLA Ops:
  0.0 60.5 %fused.1 = bf16[256,5120]{1,0:T(8,128)(2,1)S(1)} custom-call(bf16[256,5120]{1,0:T(8,128)(2,1)} %key_ref.1, bf16[256,5120]{1,0:T(8,128)(2,1)} %value_ref.1, bf16[256,5120]{1,0:T(8,128)(2,1)} %query_hbm.1, s32[20,512]{1,0:T(8,128)} %perm_hbm.1, s32[20,4,64]{2,1,0:T(4,128)} %mask_hbm.1), custom_call_target="tpu_custom_call" | custom-call | tf_op jit(solution)/shard_map/fused/pallas_call | solution.py:581
  60.5 1.5 %copy.7 = bf16[256,5120]{1,0:T(8,128)(2,1)} copy(bf16[256,5120]{1,0:T(8,128)(2,1)S(1)} %fused.1) | data formatting | bytes 5242880

commit v3 on v0

--- a/solution.py
+++ b/solution.py
@@ -248,6 +248,417 @@
     stay.wait()
 
 
+def request(shard_blocks, capacity, mask_ref, tab_ref):
+    heads, _, blocks = mask_ref.shape
+    seq_count = blocks // shard_blocks
+    needed = jnp.max(mask_ref[...], axis=1).astype(jnp.float32)
+    row, col = iota((blocks, blocks), 0), iota((blocks, blocks), 1)
+    same = (row // shard_blocks) == (col // shard_blocks)
+    small = lambda value: value.astype(jnp.float32).astype(jnp.bfloat16)
+    dot = functools.partial(jnp.dot, preferred_element_type=jnp.float32)
+    by_owner = dot(small(needed), small(same))
+    lower = small(iota((heads, heads), 1) < iota((heads, heads), 0))
+    rank = dot(lower, small(by_owner)) + dot(small(needed), small(same & (row < col)))
+    head_ids, block_ids = iota((heads, blocks), 0), iota((heads, blocks), 1)
+    pair = (block_ids % shard_blocks * heads + head_ids).astype(jnp.float32)
+    slot_row = iota((128, blocks), 0)
+    sums = jnp.zeros((128, blocks), jnp.float32)
+    for c in range(capacity):
+        taken = (rank == c) & (needed > 0.5)
+        for lane, value in ((2 * c, pair), (2 * c + 1, head_ids.astype(jnp.float32))):
+            hit = jnp.sum(jnp.where(taken, value, 0.0), axis=0, keepdims=True)
+            sums = jnp.where(slot_row == lane, hit, sums)
+    owner_t = small(iota((seq_count, blocks), 1) // shard_blocks == iota((seq_count, blocks), 0))
+    asked = lax.dot_general(
+        owner_t, small(sums), (((1,), (1,)), ((), ())), preferred_element_type=jnp.float32
+    )
+    tab_ref[:seq_count] = (asked + 0.5).astype(jnp.int32)[:, None, :]
+    spot = (block_ids // shard_blocks * capacity).astype(jnp.float32) + rank
+    spot = jnp.sum(jnp.where(needed > 0.5, spot, 0.0), axis=1, keepdims=True)
+    spot = (jnp.broadcast_to(spot, (heads, 128)) + 0.5).astype(jnp.int32)
+    tab_ref[seq_count:] = spot[:, None, :]
+
+
+def fused_kernel(
+    seq_count, capacity, shard_blocks,
+    key_ref, value_ref, query_hbm, perm_hbm, mask_hbm, stage_ref, tab_ref, far_tab_ref,
+    perm_ref, mask_ref, keys, values, query_ref, send_ref, got_ref, asked_ref, rows_ref, blocks_ref,
+    own_tab, far_tab, asked_near, asked,
+    near_sem, load_sem, swap_send, swap_recv, ask_send, ask_recv, misc_sem,
+    send_sem, recvs, relay_send, relay_recv, step_sem,
+):
+    group, me = lax.axis_index("head"), lax.axis_index("seq")
+    other = 1 - group
+    heads = perm_ref.shape[0]
+    rows = query_hbm.shape[0]
+    half = heads * HEAD_DIM
+    spread = seq_count // 4
+    peer_of = lambda step: partner_of(me, step, seq_count)
+    top, low = (me // (2 * spread)) % 2, (me // spread) % 2
+    edge = (top + low + 1) % 2
+
+    def near_peer(i):
+        far = (3 - i) // 2
+        turn = edge * ((i + 1) // 2) + (1 - edge) * ((i + 1) % 2)
+        return peer_of(spread * (2 * far + turn))
+
+    def side_peer(plane, k):
+        return peer_of(spread * plane + 1 + k)
+
+    def far_peer(k):
+        plane = 2 + edge * ((k + 1) % 2) + (1 - edge) * (k % 2)
+        return side_peer(plane, k // 2)
+
+    def times(count, body):
+        lax.fori_loop(0, count, lambda i, carry: (body(i), carry)[1], 0)
+
+    beside = spread - 1
+
+    def all_rest(body):
+        times(beside, lambda k: body(side_peer(0, k)))
+        times(beside, lambda k: body(side_peer(1, k)))
+        times(2 * beside, lambda k: body(far_peer(k)))
+
+    barrier = pltpu.get_barrier_semaphore()
+    pl.semaphore_signal(barrier, inc=1, device_id={"head": other}, device_id_type=MESH)
+    for step in (spread, 2 * spread, 3 * spread, 1, 2):
+        pl.semaphore_signal(barrier, inc=1, device_id={"seq": peer_of(step)}, device_id_type=MESH)
+
+    masks = pltpu.make_async_copy(mask_hbm, mask_ref, misc_sem.at[0])
+    masks.start()
+    perms = pltpu.make_async_copy(perm_hbm, perm_ref, misc_sem.at[1])
+    perms.start()
+    here = pl.ds(pl.multiple_of(group * rows, rows), rows)
+    sides = ((key_ref, keys), (value_ref, values))
+
+    def load(number, start_at, span):
+        src, dst = sides[number]
+        mine = pl.ds(pl.multiple_of(group * half + start_at, HEAD_DIM), span)
+        return pltpu.make_async_copy(
+            src.at[:, mine], dst.at[here, pl.ds(start_at, span)], load_sem.at[number]
+        )
+
+    def swap(number, start_at, span):
+        src, dst = sides[number]
+        theirs = pl.ds(pl.multiple_of(other * half + start_at, HEAD_DIM), span)
+        return pltpu.make_async_remote_copy(
+            src_ref=src.at[:, theirs], dst_ref=dst.at[here, pl.ds(start_at, span)],
+            send_sem=swap_send.at[number], recv_sem=swap_recv.at[number],
+            device_id={"head": other}, device_id_type=MESH,
+        )
+
+    parts = 4
+    cuts = [(number, part * (half // parts), half // parts) for number in range(2) for part in range(parts)]
+    for cut in cuts[:parts]:
+        load(*cut).start()
+    take = pltpu.make_async_copy(query_hbm, query_ref, misc_sem.at[2])
+    masks.wait()
+    request(shard_blocks, capacity, mask_ref, tab_ref)
+    pl.semaphore_wait(barrier, 6)
+
+    def ask(peer, landing, near):
+        return pltpu.make_async_remote_copy(
+            src_ref=tab_ref.at[peer], dst_ref=asked_ref.at[peer if landing else me],
+            send_sem=ask_send.at[0],
+            recv_sem=ask_recv.at[near * (1 + (peer if landing else me) // spread)],
+            device_id={"seq": peer}, device_id_type=MESH,
+        )
+
+    def asks(count):
+        return pltpu.make_async_remote_copy(
+            src_ref=tab_ref.at[pl.ds(0, count)], dst_ref=asked_ref.at[pl.ds(0, count)],
+            send_sem=ask_send.at[0], recv_sem=ask_recv.at[0],
+            device_id={"head": other}, device_id_type=MESH,
+        )
+
+    times(3, lambda i: ask(near_peer(i), False, 1).start())
+    for cut in cuts:
+        swap(*cut).start()
+    for cut in cuts[parts:]:
+        load(*cut).start()
+    for number, step in enumerate((1, 2)):
+        pl.semaphore_signal(
+            step_sem.at[number], inc=1, device_id={"seq": peer_of(step)}, device_id_type=MESH
+        )
+    tell = pltpu.make_async_remote_copy(
+        src_ref=tab_ref, dst_ref=far_tab_ref, send_sem=misc_sem.at[3], recv_sem=misc_sem.at[4],
+        device_id={"head": other}, device_id_type=MESH,
+    )
+    tell.start()
+    keep = pltpu.make_async_copy(tab_ref.at[me], asked_ref.at[me], misc_sem.at[5])
+    keep.start()
+    own = pltpu.make_async_copy(tab_ref, own_tab, misc_sem.at[6])
+    own.start()
+    perms.wait()
+    for b in range(shard_blocks):
+        blocks_ref[b * heads : (b + 1) * heads] = perm_ref[:, b * BLOCK : (b + 1) * BLOCK][:, None, :]
+    rows_ref[...] = jnp.zeros_like(rows_ref)
+
+    def near_scalar(peer):
+        return pltpu.make_async_copy(
+            asked_ref.at[peer], asked_near.at[peer], near_sem.at[peer // spread]
+        )
+
+    pl.semaphore_wait(step_sem.at[0], 1)
+    pl.semaphore_wait(step_sem.at[1], 1)
+    pl.semaphore_signal(step_sem.at[2], inc=1, device_id={"seq": peer_of(2)}, device_id_type=MESH)
+
+    token = iota((BLOCK, 2 * rows), 1) + me * (2 * rows)
+
+    def gather(table_ref, peer, whiches, put):
+        chosen = []
+        for c in range(capacity):
+            pair = jnp.clip(table_ref[peer, 0, 2 * c], 0, heads * shard_blocks - 1)
+            rows_ref[c : c + 1, :] = blocks_ref[pair]
+            head = jnp.clip(table_ref[peer, 0, 2 * c + 1], 0, heads - 1)
+            chosen.append(head * HEAD_DIM)
+        turned = rows_ref[...].T
+        for c, start_at in enumerate(chosen):
+            table = (turned[:, c : c + 1] == token).astype(jnp.float32).astype(jnp.bfloat16)
+            for which in whiches:
+                got = jnp.dot(
+                    table, sides[which][1][:, pl.ds(start_at, HEAD_DIM)],
+                    preferred_element_type=jnp.float32,
+                )
+                put(which, c, got.astype(jnp.bfloat16))
+
+    def to_send(peer):
+        def put(which, c, got):
+            send_ref[peer, which, c] = got
+
+        return put
+
+    def near_deliver(which, peer):
+        return pltpu.make_async_remote_copy(
+            src_ref=send_ref.at[peer, which], dst_ref=got_ref.at[0, me, which],
+            send_sem=send_sem.at[0], recv_sem=recvs.at[me],
+            device_id={"seq": peer}, device_id_type=MESH,
+        )
+
+    def deliver(peer, landing):
+        source = peer if landing else me
+        return pltpu.make_async_remote_copy(
+            src_ref=send_ref.at[peer], dst_ref=got_ref.at[0, source],
+            send_sem=send_sem.at[0], recv_sem=recvs.at[source],
+            device_id={"seq": peer}, device_id_type=MESH,
+        )
+
+    def relay(source):
+        return pltpu.make_async_remote_copy(
+            src_ref=got_ref.at[0, source], dst_ref=got_ref.at[1, source],
+            send_sem=relay_send.at[0], recv_sem=relay_recv.at[source],
+            device_id={"head": other}, device_id_type=MESH,
+        )
+
+    def serve(i, which):
+        peer = near_peer(i)
+        if which == 0:
+            near_scalar(peer).wait()
+        gather(asked_near, peer, (which,), to_send(peer))
+        near_deliver(which, peer).start()
+
+    def heed(i):
+        peer = near_peer(i)
+        ask(peer, True, 1).wait_recv()
+        near_scalar(peer).start()
+
+    load(0, 0, half).wait()
+    heed(0)
+    pl.semaphore_wait(step_sem.at[2], 1)
+    all_rest(lambda peer: ask(peer, False, 0).start())
+    heed(1)
+    swap(0, 0, half).wait_recv()
+    serve(0, 0)
+    serve(1, 0)
+    heed(2)
+    serve(2, 0)
+    load(1, 0, half).wait()
+    swap(1, 0, half).wait_recv()
+    times(3, lambda i: serve(i, 1))
+    take.start()
+    own.wait()
+    tell.wait_recv()
+    far_scalar = pltpu.make_async_copy(far_tab_ref, far_tab, misc_sem.at[8])
+    far_scalar.start()
+
+    def to_got(which, c, got):
+        got_ref[0, me, which, c] = got
+
+    gather(own_tab, me, (0, 1), to_got)
+    relay(me).start()
+    keep.wait()
+    asks(seq_count - 4).wait_recv()
+    to_scalar = pltpu.make_async_copy(asked_ref, asked, misc_sem.at[7])
+    to_scalar.start()
+    to_scalar.wait()
+
+    def produce(i):
+        far = edge * ((i + 2 * beside) // (3 * beside)) + (1 - edge) * ((5 * beside - 1 - i) // (3 * beside))
+        at = i - beside * edge + 3 * beside * (1 - far)
+        peer = far * far_peer(at % (3 * beside)) + (1 - far) * side_peer(1, at % beside)
+        gather(asked, peer, (0, 1), to_send(peer))
+        deliver(peer, False).start()
+
+    def produce_beside(k):
+        peer = side_peer(0, k)
+        gather(asked, peer, (0, 1), to_send(peer))
+        deliver(peer, False).start()
+
+    times(3 * beside, produce)
+    times(beside, produce_beside)
+    far_scalar.wait()
+    take.wait()
+
+    scale = math.log2(math.e) / math.sqrt(HEAD_DIM)
+    ones = jnp.ones((BLOCK, HEAD_DIM), jnp.bfloat16)
+
+    def attend(items):
+        scores = []
+        for rel, source, c in items:
+            tab, base = ((own_tab, group), (far_tab, other))[rel]
+            head = base * heads + jnp.clip(tab[source, 0, 2 * c + 1], 0, heads - 1)
+            query = query_ref[:, pl.ds(head * HEAD_DIM, HEAD_DIM)]
+            scores.append(
+                lax.dot_general(
+                    query, got_ref[rel, source, 0, c], (((1,), (1,)), ((), ())),
+                    preferred_element_type=jnp.float32,
+                )
+            )
+        weights = []
+        for score in scores:
+            peak = jnp.max(score, axis=1, keepdims=True)
+            weights.append(jnp.exp2((score - peak) * scale).astype(jnp.bfloat16))
+        for (rel, source, c), weight in zip(items, weights):
+            mixed = jnp.dot(
+                weight, jnp.concatenate([got_ref[rel, source, 1, c], ones], axis=1),
+                preferred_element_type=jnp.float32,
+            )
+            stage_ref[rel, source * capacity + c] = (
+                mixed[:, :HEAD_DIM] / mixed[:, HEAD_DIM:]
+            ).astype(jnp.bfloat16)
+
+    slots = lambda rel, source: [(rel, source, c) for c in range(capacity)]
+    attend(slots(0, me))
+    relay(me).wait_recv()
+    attend(slots(1, me))
+
+    def near_take(i):
+        source = near_peer(i)
+        deliver(source, True).wait_recv()
+        relay(source).start()
+
+    times(3, near_take)
+
+    def near_use(i):
+        source = near_peer(i)
+        relay(source).wait_recv()
+        attend(slots(0, source) + slots(1, source))
+
+    times(3, near_use)
+
+    def rest_peer(i):
+        late = i // (2 * beside)
+        plane = (1 - late) * (i // beside) + late * (2 + i % 2)
+        return side_peer(plane, (1 - late) * (i % beside) + late * (i % (2 * beside) // 2))
+
+    def use(i, first=False, last=False):
+        before = [] if first else [rest_peer(2 * i - 2), rest_peer(2 * i - 1)]
+        sources = [] if last else [rest_peer(2 * i), rest_peer(2 * i + 1)]
+        for source in sources:
+            deliver(source, True).wait_recv()
+            relay(source).start()
+        for source in before:
+            relay(source).wait_recv()
+        items = [slots(0, source) for source in sources] + [slots(1, source) for source in before]
+        attend(sum(items, []))
+
+    pairs = 2 * beside
+    use(0, first=True)
+    times(pairs - 1, lambda i: use(i + 1))
+    use(pairs, last=True)
+
+    for number in range(2):
+        swap(number, 0, half).wait_send()
+    asks(seq_count - 1).wait_send()
+    tell.wait_send()
+    pltpu.make_async_remote_copy(
+        src_ref=send_ref.at[pl.ds(0, seq_count - 1)], dst_ref=got_ref.at[0, pl.ds(0, seq_count - 1)],
+        send_sem=send_sem.at[0], recv_sem=recvs.at[me],
+        device_id={"head": other}, device_id_type=MESH,
+    ).wait_send()
+    pltpu.make_async_remote_copy(
+        src_ref=got_ref.at[0], dst_ref=got_ref.at[1],
+        send_sem=relay_send.at[0], recv_sem=relay_recv.at[me],
+        device_id={"head": other}, device_id_type=MESH,
+    ).wait_send()
+
+
+def flush_kernel(seq_count, stage_ref, tab_ref, far_tab_ref, out_ref, sem):
+    group = lax.axis_index("head")
+    heads = tab_ref.shape[0] - seq_count
+    last = stage_ref.shape[1] - 1
+    for local in range(heads):
+        for rel, (tab, base) in enumerate(((tab_ref, group), (far_tab_ref, 1 - group))):
+            slot = jnp.clip(tab[seq_count + local, 0, 0], 0, last)
+            at = pl.multiple_of((base * heads + local) * HEAD_DIM, HEAD_DIM)
+            pltpu.make_async_copy(
+                stage_ref.at[rel, slot], out_ref.at[:, pl.ds(at, HEAD_DIM)], sem.at[0]
+            ).start()
+    pltpu.make_async_copy(out_ref, out_ref, sem.at[0]).wait()
+
+
+def fused(key_states, value_states, queries, cluster_perm, block_mask, capacity):
+    heads, shard_rows = cluster_perm.shape
+    shard_blocks = shard_rows // BLOCK
+    seq_count = lax.axis_size("seq")
+    rows, columns = queries.shape
+    vmem = pl.BlockSpec(memory_space=pltpu.VMEM)
+    anywhere = pl.BlockSpec(memory_space=pltpu.HBM)
+    bf16, i32 = jnp.bfloat16, jnp.int32
+    dma = pltpu.SemaphoreType.DMA
+    resident = 4 * seq_count * capacity * rows * HEAD_DIM + 8 * 8 * 128 * (seq_count + heads)
+    table, asks = (seq_count + heads, 1, 128), (seq_count, 1, 128)
+    staged = pl.pallas_call(
+        functools.partial(fused_kernel, seq_count, capacity, shard_blocks),
+        out_shape=(
+            pltpu.VMEM((2, seq_count * capacity, rows, HEAD_DIM), bf16),
+            pltpu.VMEM(table, i32), pltpu.VMEM(table, i32),
+        ),
+        in_specs=[anywhere] * 5,
+        out_specs=(vmem, vmem, vmem),
+        scratch_shapes=[
+            pltpu.VMEM(cluster_perm.shape, i32), pltpu.VMEM(block_mask.shape, i32),
+            pltpu.VMEM((shard_rows, heads * HEAD_DIM), bf16),
+            pltpu.VMEM((shard_rows, heads * HEAD_DIM), bf16),
+            pltpu.VMEM((rows, columns), bf16),
+            pltpu.VMEM((seq_count, 2, capacity, BLOCK, HEAD_DIM), bf16),
+            pltpu.VMEM((2, seq_count, 2, capacity, BLOCK, HEAD_DIM), bf16),
+            pltpu.VMEM(asks, i32),
+            pltpu.VMEM((8 * -(-capacity // 8), 128), i32),
+            pltpu.VMEM((shard_blocks * heads, 1, BLOCK), i32),
+            pltpu.SMEM(table, i32), pltpu.SMEM(table, i32),
+            pltpu.SMEM(asks, i32), pltpu.SMEM(asks, i32),
+            dma((4,)), dma((2,)), dma((2,)), dma((2,)), dma((1,)), dma((5,)), dma((9,)),
+            dma((1,)), dma((seq_count,)), dma((1,)), dma((seq_count,)),
+            pltpu.SemaphoreType.REGULAR((3,)),
+        ],
+        compiler_params=pltpu.CompilerParams(
+            collective_id=1, has_side_effects=True,
+            vmem_limit_bytes=67043328 - resident - 256 * 1024,
+        ),
+        name="fused",
+    )(key_states, value_states, queries, cluster_perm, block_mask)
+    return pl.pallas_call(
+        functools.partial(flush_kernel, seq_count),
+        out_shape=jax.ShapeDtypeStruct((rows, columns), bf16),
+        in_specs=[vmem, vmem, vmem],
+        out_specs=anywhere,
+        scratch_shapes=[dma((1,))],
+        compiler_params=pltpu.CompilerParams(vmem_limit_bytes=8 * 1024 * 1024),
+        name="flush",
+    )(*staged)
+
+
 def attend_kernel(heads, picks, width, capacity, masked, pos_own, pos_far, *refs):
     if masked:
         query_ref, kv_ref, allow_ref, out_ref, stage, sems = refs
@@ -347,6 +758,8 @@
     )
     rows, columns = queries.shape
     me = lax.axis_index("seq")
+    if picks == 1 and seq_count == 16 and shard_blocks * group_heads <= 256:
+        return fused(key_states, value_states, queries, cluster_perm, block_mask, capacity)
     vmem = pl.BlockSpec(memory_space=pltpu.VMEM)
     anywhere = pl.BlockSpec(memory_space=pltpu.HBM)
     struct = jax.ShapeDtypeStruct

time: 73.1 us -> 59.8 us (0.82)
  Pallas kernels: 71.2 us -> 58.9 us
  local copies, waits for them, and re-layouts: 1.41 us -> 0 us
    pallas_call x2, Pallas kernels: 71.2 us -> 58.9 us  [the longest x1 57.4 us: fused(): pl.pallas_call(functools.partial(fused_kernel, seq_count, capacity, shard...]
    unnamed x4 -> x0, local copies, waits for them, and re-layouts: 1.41 us -> none
where the time goes in v3:
time: 59.8 us; the launch traced here: 59 us
  Pallas kernels  58.9 us (98%)
    pallas_call x1, Pallas kernels, fused(): pl.pallas_call(functools.partial(fused_kernel, seq_count, capacity, shard...  57.4 us
    pallas_call x1, Pallas kernels, fused(): pl.pallas_call(functools.partial(flush_kernel, seq_count), out_shape=jax....  1.53 us

profile of v3, /device:TPU:1, one launch (start us, length us, event | category | flops | bytes accessed | tf_op | source)
XLA Modules:
  0.0 59.0 jit_solution(5601963250371371213)
XLA Ops:
  0.0 57.4 %fused.1 = (bf16[2,32,256,128]{3,2,1,0:T(8,128)(2,1)S(1)}, s32[36,1,128]{2,1,0:T(1,128)S(1)}, s32[36,1,128]{2,1,0:T(1,128)S(1)}) custom-call(bf16[256,5120]{1,0:T(8,128)(2,1)} %key_ref.1, bf16[256,5120]{1,0:T(8,128)(2,1)} %value_ref.1, bf16[256,5120]{1,0:T(8,128)(2,1)} %query_hbm.1, s32[20,512]{1,0:T(8,128)} %perm_hbm.1, s32[20,4,64]{2,1,0:T(4,128)} %mask_hbm.1), custom_call_target="tpu_custom_call" | custom-call | tf_op jit(solution)/shard_map/fused/pallas_call | solution.py:621
  57.4 1.5 %flush.1 = bf16[256,5120]{1,0:T(8,128)(2,1)} custom-call(bf16[2,32,256,128]{3,2,1,0:T(8,128)(2,1)S(1)} %get-tuple-element.8.stage_ref, s32[36,1,128]{2,1,0:T(1,128)S(1)} %get-tuple-element.9.tab_ref, s32[36,1,128]{2,1,0:T(1,128)S(1)} %get-tuple-element.10.far_tab_ref), custom_call_target="tpu_custom_call" | custom-call | tf_op jit(solution)/shard_map/flush/pallas_call | solution.py:651

commit v4 on v3

--- a/solution.py
+++ b/solution.py
@@ -306,8 +306,7 @@
         return peer_of(spread * plane + 1 + k)
 
     def far_peer(k):
-        plane = 2 + edge * ((k + 1) % 2) + (1 - edge) * (k % 2)
-        return side_peer(plane, k // 2)
+        return side_peer(2 + (edge + (1 - top) * (1 - group) + k) % 2, k // 2)
 
     def times(count, body):
         lax.fori_loop(0, count, lambda i, carry: (body(i), carry)[1], 0)

time: 59.8 us -> 59.1 us (0.988); the launches traced: 59 us -> 59 us
  no operation moved by 1% of the time
where the time goes in v4:
time: 59.1 us; the launch traced here: 59 us
  Pallas kernels  58.9 us (100%)
    pallas_call x1, Pallas kernels, fused(): pl.pallas_call(functools.partial(fused_kernel, seq_count, capacity, shard...  57.4 us
    pallas_call x1, Pallas kernels, fused(): pl.pallas_call(functools.partial(flush_kernel, seq_count), out_shape=jax....  1.53 us

profile of v4, /device:TPU:1, one launch (start us, length us, event | category | flops | bytes accessed | tf_op | source)
XLA Modules:
  0.0 59.0 jit_solution(5254491295541889890)
XLA Ops:
  0.0 57.4 %fused.1 = (bf16[2,32,256,128]{3,2,1,0:T(8,128)(2,1)S(1)}, s32[36,1,128]{2,1,0:T(1,128)S(1)}, s32[36,1,128]{2,1,0:T(1,128)S(1)}) custom-call(bf16[256,5120]{1,0:T(8,128)(2,1)} %key_ref.1, bf16[256,5120]{1,0:T(8,128)(2,1)} %value_ref.1, bf16[256,5120]{1,0:T(8,128)(2,1)} %query_hbm.1, s32[20,512]{1,0:T(8,128)} %perm_hbm.1, s32[20,4,64]{2,1,0:T(4,128)} %mask_hbm.1), custom_call_target="tpu_custom_call" | custom-call | tf_op jit(solution)/shard_map/fused/pallas_call | solution.py:620
  57.4 1.5 %flush.1 = bf16[256,5120]{1,0:T(8,128)(2,1)} custom-call(bf16[2,32,256,128]{3,2,1,0:T(8,128)(2,1)S(1)} %get-tuple-element.8.stage_ref, s32[36,1,128]{2,1,0:T(1,128)S(1)} %get-tuple-element.9.tab_ref, s32[36,1,128]{2,1,0:T(1,128)S(1)} %get-tuple-element.10.far_tab_ref), custom_call_target="tpu_custom_call" | custom-call | tf_op jit(solution)/shard_map/flush/pallas_call | solution.py:650

commit v5 on v4

--- a/solution.py
+++ b/solution.py
@@ -305,8 +305,11 @@
     def side_peer(plane, k):
         return peer_of(spread * plane + 1 + k)
 
+    def turn_of(k):
+        return 3 + k * (2 - 3) + k * (k - 1) // 2 * (1 - 2 * 2 + 3) - 1
+
     def far_peer(k):
-        return side_peer(2 + (edge + (1 - top) * (1 - group) + k) % 2, k // 2)
+        return side_peer(2 + (edge + (1 - top) * (1 - group) + k) % 2, turn_of(k // 2))
 
     def times(count, body):
         lax.fori_loop(0, count, lambda i, carry: (body(i), carry)[1], 0)
@@ -503,8 +506,8 @@
         gather(asked, peer, (0, 1), to_send(peer))
         deliver(peer, False).start()
 
+    times(beside, produce_beside)
     times(3 * beside, produce)
-    times(beside, produce_beside)
     far_scalar.wait()
     take.wait()
 
@@ -558,7 +561,7 @@
     def rest_peer(i):
         late = i // (2 * beside)
         plane = (1 - late) * (i // beside) + late * (2 + i % 2)
-        return side_peer(plane, (1 - late) * (i % beside) + late * (i % (2 * beside) // 2))
+        return side_peer(plane, (1 - late) * (i % beside) + late * turn_of(i % (2 * beside) // 2))
 
     def use(i, first=False, last=False):
         before = [] if first else [rest_peer(2 * i - 2), rest_peer(2 * i - 1)]

time: 59.1 us -> 58.1 us (0.983)
  Pallas kernels: 58.9 us -> 58 us
    pallas_call x1, Pallas kernels: 57.4 us -> 56.5 us  [fused(): pl.pallas_call(functools.partial(fused_kernel, seq_count, capacity, shard...]
where the time goes in v5:
time: 58.1 us; the launch traced here: 58 us
  Pallas kernels  58 us (100%)
    pallas_call x1, Pallas kernels, fused(): pl.pallas_call(functools.partial(fused_kernel, seq_count, capacity, shard...  56.5 us
    pallas_call x1, Pallas kernels, fused(): pl.pallas_call(functools.partial(flush_kernel, seq_count), out_shape=jax....  1.53 us

profile of v5, /device:TPU:1, one launch (start us, length us, event | category | flops | bytes accessed | tf_op | source)
XLA Modules:
  0.0 58.0 jit_solution(16896280042786278830)
XLA Ops:
  0.0 56.5 %fused.1 = (bf16[2,32,256,128]{3,2,1,0:T(8,128)(2,1)S(1)}, s32[36,1,128]{2,1,0:T(1,128)S(1)}, s32[36,1,128]{2,1,0:T(1,128)S(1)}) custom-call(bf16[256,5120]{1,0:T(8,128)(2,1)} %key_ref.1, bf16[256,5120]{1,0:T(8,128)(2,1)} %value_ref.1, bf16[256,5120]{1,0:T(8,128)(2,1)} %query_hbm.1, s32[20,512]{1,0:T(8,128)} %perm_hbm.1, s32[20,4,64]{2,1,0:T(4,128)} %mask_hbm.1), custom_call_target="tpu_custom_call" | custom-call | tf_op jit(solution)/shard_map/fused/pallas_call | solution.py:623
  56.5 1.5 %flush.1 = bf16[256,5120]{1,0:T(8,128)(2,1)} custom-call(bf16[2,32,256,128]{3,2,1,0:T(8,128)(2,1)S(1)} %get-tuple-element.8.stage_ref, s32[36,1,128]{2,1,0:T(1,128)S(1)} %get-tuple-element.9.tab_ref, s32[36,1,128]{2,1,0:T(1,128)S(1)} %get-tuple-element.10.far_tab_ref), custom_call_target="tpu_custom_call" | custom-call | tf_op jit(solution)/shard_map/flush/pallas_call | solution.py:653

commit v6 on v5

--- a/solution.py
+++ b/solution.py
@@ -282,9 +282,9 @@
 def fused_kernel(
     seq_count, capacity, shard_blocks,
     key_ref, value_ref, query_hbm, perm_hbm, mask_hbm, stage_ref, tab_ref, far_tab_ref,
-    perm_ref, mask_ref, keys, values, query_ref, send_ref, got_ref, asked_ref, rows_ref, blocks_ref,
-    own_tab, far_tab, asked_near, asked,
-    near_sem, load_sem, swap_send, swap_recv, ask_send, ask_recv, misc_sem,
+    perm_ref, mask_ref, keys, values, query_ref, send_ref, got_ref, rows_ref, blocks_ref,
+    own_tab, far_tab, asked,
+    load_sem, swap_send, swap_recv, ask_send, ask_recv, misc_sem,
     send_sem, recvs, relay_send, relay_recv, step_sem,
 ):
     group, me = lax.axis_index("head"), lax.axis_index("seq")
@@ -316,15 +316,18 @@
 
     beside = spread - 1
 
-    def all_rest(body):
-        times(beside, lambda k: body(side_peer(0, k)))
-        times(beside, lambda k: body(side_peer(1, k)))
-        times(2 * beside, lambda k: body(far_peer(k)))
-
     barrier = pltpu.get_barrier_semaphore()
     pl.semaphore_signal(barrier, inc=1, device_id={"head": other}, device_id_type=MESH)
-    for step in (spread, 2 * spread, 3 * spread, 1, 2):
-        pl.semaphore_signal(barrier, inc=1, device_id={"seq": peer_of(step)}, device_id_type=MESH)
+
+    def signal(sem, step):
+        pl.semaphore_signal(sem, inc=1, device_id={"seq": peer_of(step)}, device_id_type=MESH)
+
+    for step in (spread, 2 * spread, 1, 2):
+        signal(barrier, step)
+
+    @pl.when(edge == 0)
+    def _():
+        signal(barrier, 3 * spread)
 
     masks = pltpu.make_async_copy(mask_hbm, mask_ref, misc_sem.at[0])
     masks.start()
@@ -356,39 +359,41 @@
     take = pltpu.make_async_copy(query_hbm, query_ref, misc_sem.at[2])
     masks.wait()
     request(shard_blocks, capacity, mask_ref, tab_ref)
-    pl.semaphore_wait(barrier, 6)
-
-    def ask(peer, landing, near):
+    pl.semaphore_wait(barrier, 6 - edge)
+
+    def ask(peer, landing, near, last=0):
         return pltpu.make_async_remote_copy(
-            src_ref=tab_ref.at[peer], dst_ref=asked_ref.at[peer if landing else me],
+            src_ref=tab_ref.at[peer], dst_ref=asked.at[peer if landing else me],
             send_sem=ask_send.at[0],
-            recv_sem=ask_recv.at[near * (1 + (peer if landing else me) // spread)],
+            recv_sem=ask_recv.at[near * (1 + (peer if landing else me) // spread) + last * 5],
             device_id={"seq": peer}, device_id_type=MESH,
         )
 
     def asks(count):
         return pltpu.make_async_remote_copy(
-            src_ref=tab_ref.at[pl.ds(0, count)], dst_ref=asked_ref.at[pl.ds(0, count)],
+            src_ref=tab_ref.at[pl.ds(0, count)], dst_ref=asked.at[pl.ds(0, count)],
             send_sem=ask_send.at[0], recv_sem=ask_recv.at[0],
             device_id={"head": other}, device_id_type=MESH,
         )
 
-    times(3, lambda i: ask(near_peer(i), False, 1).start())
+    ask(peer_of(2 * spread), False, 1).start()
+    ask(peer_of(spread), False, 1).start()
+
+    @pl.when(edge == 0)
+    def _():
+        ask(peer_of(3 * spread), False, 1).start()
+
     for cut in cuts:
         swap(*cut).start()
     for cut in cuts[parts:]:
         load(*cut).start()
-    for number, step in enumerate((1, 2)):
-        pl.semaphore_signal(
-            step_sem.at[number], inc=1, device_id={"seq": peer_of(step)}, device_id_type=MESH
-        )
+    for number, step in enumerate((1, 2, spread)):
+        signal(step_sem.at[number], step)
     tell = pltpu.make_async_remote_copy(
         src_ref=tab_ref, dst_ref=far_tab_ref, send_sem=misc_sem.at[3], recv_sem=misc_sem.at[4],
         device_id={"head": other}, device_id_type=MESH,
     )
     tell.start()
-    keep = pltpu.make_async_copy(tab_ref.at[me], asked_ref.at[me], misc_sem.at[5])
-    keep.start()
     own = pltpu.make_async_copy(tab_ref, own_tab, misc_sem.at[6])
     own.start()
     perms.wait()
@@ -396,14 +401,20 @@
         blocks_ref[b * heads : (b + 1) * heads] = perm_ref[:, b * BLOCK : (b + 1) * BLOCK][:, None, :]
     rows_ref[...] = jnp.zeros_like(rows_ref)
 
-    def near_scalar(peer):
-        return pltpu.make_async_copy(
-            asked_ref.at[peer], asked_near.at[peer], near_sem.at[peer // spread]
-        )
-
-    pl.semaphore_wait(step_sem.at[0], 1)
-    pl.semaphore_wait(step_sem.at[1], 1)
-    pl.semaphore_signal(step_sem.at[2], inc=1, device_id={"seq": peer_of(2)}, device_id_type=MESH)
+    def ask_far(*places):
+        for plane, turn in places:
+            ask(peer_of(spread * plane + turn), False, 0).start()
+
+    for number in range(3):
+        pl.semaphore_wait(step_sem.at[number], 1)
+    for number, step in enumerate((1, 2)):
+        signal(step_sem.at[3 + number], step)
+
+    @pl.when(edge == 1)
+    def _():
+        ask(peer_of(3 * spread), False, 1).start()
+
+    ask_far((2, 1), (2, 2), (1, 1), (1, 2), (0, 1), (0, 2), (0, 3))
 
     token = iota((BLOCK, 2 * rows), 1) + me * (2 * rows)
 
@@ -454,23 +465,34 @@
 
     def serve(i, which):
         peer = near_peer(i)
-        if which == 0:
-            near_scalar(peer).wait()
-        gather(asked_near, peer, (which,), to_send(peer))
+        gather(asked, peer, (which,), to_send(peer))
         near_deliver(which, peer).start()
 
     def heed(i):
         peer = near_peer(i)
         ask(peer, True, 1).wait_recv()
-        near_scalar(peer).start()
 
     load(0, 0, half).wait()
     heed(0)
-    pl.semaphore_wait(step_sem.at[2], 1)
-    all_rest(lambda peer: ask(peer, False, 0).start())
-    heed(1)
+    pl.semaphore_wait(step_sem.at[3], 1)
+    pl.semaphore_wait(step_sem.at[4], 1)
+    signal(step_sem.at[5], 2)
+    ask_far((2, 3), (3, 1), (3, 2), (1, 3))
+    remotest = peer_of(3 * spread + 3)
+
+    @pl.when(edge == 0)
+    def _():
+        ask(remotest, False, 0, 1).start()
+
     swap(0, 0, half).wait_recv()
     serve(0, 0)
+    pl.semaphore_wait(step_sem.at[5], 1)
+
+    @pl.when(edge == 1)
+    def _():
+        ask(remotest, False, 0, 1).start()
+
+    heed(1)
     serve(1, 0)
     heed(2)
     serve(2, 0)
@@ -488,26 +510,32 @@
 
     gather(own_tab, me, (0, 1), to_got)
     relay(me).start()
-    keep.wait()
-    asks(seq_count - 4).wait_recv()
-    to_scalar = pltpu.make_async_copy(asked_ref, asked, misc_sem.at[7])
-    to_scalar.start()
-    to_scalar.wait()
+    asks(seq_count - 5).wait_recv()
 
     def produce(i):
         far = edge * ((i + 2 * beside) // (3 * beside)) + (1 - edge) * ((5 * beside - 1 - i) // (3 * beside))
         at = i - beside * edge + 3 * beside * (1 - far)
-        peer = far * far_peer(at % (3 * beside)) + (1 - far) * side_peer(1, at % beside)
+        peer = far * far_peer(at % (3 * beside)) + (1 - far) * side_peer(1, turn_of(at % beside))
         gather(asked, peer, (0, 1), to_send(peer))
         deliver(peer, False).start()
 
     def produce_beside(k):
-        peer = side_peer(0, k)
+        peer = side_peer(0, turn_of(k))
         gather(asked, peer, (0, 1), to_send(peer))
         deliver(peer, False).start()
 
+    @pl.when(edge == 0)
+    def _():
+        ask(remotest, True, 0, 1).wait_recv()
+
     times(beside, produce_beside)
-    times(3 * beside, produce)
+    times(beside, produce)
+
+    @pl.when(edge == 1)
+    def _():
+        ask(remotest, True, 0, 1).wait_recv()
+
+    times(2 * beside, lambda i: produce(i + beside))
     far_scalar.wait()
     take.wait()
 
@@ -561,7 +589,7 @@
     def rest_peer(i):
         late = i // (2 * beside)
         plane = (1 - late) * (i // beside) + late * (2 + i % 2)
-        return side_peer(plane, (1 - late) * (i % beside) + late * turn_of(i % (2 * beside) // 2))
+        return side_peer(plane, turn_of((1 - late) * (i % beside) + late * (i % (2 * beside) // 2)))
 
     def use(i, first=False, last=False):
         before = [] if first else [rest_peer(2 * i - 2), rest_peer(2 * i - 1)]
@@ -635,14 +663,13 @@
             pltpu.VMEM((rows, columns), bf16),
             pltpu.VMEM((seq_count, 2, capacity, BLOCK, HEAD_DIM), bf16),
             pltpu.VMEM((2, seq_count, 2, capacity, BLOCK, HEAD_DIM), bf16),
-            pltpu.VMEM(asks, i32),
             pltpu.VMEM((8 * -(-capacity // 8), 128), i32),
             pltpu.VMEM((shard_blocks * heads, 1, BLOCK), i32),
             pltpu.SMEM(table, i32), pltpu.SMEM(table, i32),
-            pltpu.SMEM(asks, i32), pltpu.SMEM(asks, i32),
-            dma((4,)), dma((2,)), dma((2,)), dma((2,)), dma((1,)), dma((5,)), dma((9,)),
+            pltpu.SMEM(asks, i32),
+            dma((2,)), dma((2,)), dma((2,)), dma((1,)), dma((6,)), dma((9,)),
             dma((1,)), dma((seq_count,)), dma((1,)), dma((seq_count,)),
-            pltpu.SemaphoreType.REGULAR((3,)),
+            pltpu.SemaphoreType.REGULAR((6,)),
         ],
         compiler_params=pltpu.CompilerParams(
             collective_id=1, has_side_effects=True,

time: 58.1 us -> 58.2 us (level)
  no operation moved by 1% of the time
where the time goes in v6:
time: 58.2 us; the launch traced here: 57.8 us
  Pallas kernels  57.8 us (99%)
    pallas_call x1, Pallas kernels, fused(): pl.pallas_call(functools.partial(fused_kernel, seq_count, capacity, shard...  56.3 us
    pallas_call x1, Pallas kernels, fused(): pl.pallas_call(functools.partial(flush_kernel, seq_count), out_shape=jax....  1.53 us

profile of v6, /device:TPU:1, one launch (start us, length us, event | category | flops | bytes accessed | tf_op | source)
XLA Modules:
  0.0 57.8 jit_solution(796053926370129037)
XLA Ops:
  0.0 56.3 %fused.1 = (bf16[2,32,256,128]{3,2,1,0:T(8,128)(2,1)S(1)}, s32[36,1,128]{2,1,0:T(1,128)S(1)}, s32[36,1,128]{2,1,0:T(1,128)S(1)}) custom-call(bf16[256,5120]{1,0:T(8,128)(2,1)} %key_ref.1, bf16[256,5120]{1,0:T(8,128)(2,1)} %value_ref.1, bf16[256,5120]{1,0:T(8,128)(2,1)} %query_hbm.1, s32[20,512]{1,0:T(8,128)} %perm_hbm.1, s32[20,4,64]{2,1,0:T(4,128)} %mask_hbm.1), custom_call_target="tpu_custom_call" | custom-call | tf_op jit(solution)/shard_map/fused/pallas_call | solution.py:651
  56.3 1.5 %flush.1 = bf16[256,5120]{1,0:T(8,128)(2,1)} custom-call(bf16[2,32,256,128]{3,2,1,0:T(8,128)(2,1)S(1)} %get-tuple-element.8.stage_ref, s32[36,1,128]{2,1,0:T(1,128)S(1)} %get-tuple-element.9.tab_ref, s32[36,1,128]{2,1,0:T(1,128)S(1)} %get-tuple-element.10.far_tab_ref), custom_call_target="tpu_custom_call" | custom-call | tf_op jit(solution)/shard_map/flush/pallas_call | solution.py:680

commit v7 on v6

--- a/solution.py
+++ b/solution.py
@@ -352,7 +352,7 @@
             device_id={"head": other}, device_id_type=MESH,
         )
 
-    parts = 4
+    parts = 1
     cuts = [(number, part * (half // parts), half // parts) for number in range(2) for part in range(parts)]
     for cut in cuts[:parts]:
         load(*cut).start()
@@ -502,7 +502,7 @@
     take.start()
     own.wait()
     tell.wait_recv()
-    far_scalar = pltpu.make_async_copy(far_tab_ref, far_tab, misc_sem.at[8])
+    far_scalar = pltpu.make_async_copy(far_tab_ref, far_tab, misc_sem.at[5])
     far_scalar.start()
 
     def to_got(which, c, got):
@@ -667,7 +667,7 @@
             pltpu.VMEM((shard_blocks * heads, 1, BLOCK), i32),
             pltpu.SMEM(table, i32), pltpu.SMEM(table, i32),
             pltpu.SMEM(asks, i32),
-            dma((2,)), dma((2,)), dma((2,)), dma((1,)), dma((6,)), dma((9,)),
+            dma((2,)), dma((2,)), dma((2,)), dma((1,)), dma((6,)), dma((7,)),
             dma((1,)), dma((seq_count,)), dma((1,)), dma((seq_count,)),
             pltpu.SemaphoreType.REGULAR((6,)),
         ],

time: 58.2 us -> 58.2 us (level)
  no operation moved by 1% of the time
where the time goes in v7:
time: 58.2 us; the launch traced here: 57.8 us
  Pallas kernels  57.8 us (99%)
    pallas_call x1, Pallas kernels, fused(): pl.pallas_call(functools.partial(fused_kernel, seq_count, capacity, shard...  56.3 us
    pallas_call x1, Pallas kernels, fused(): pl.pallas_call(functools.partial(flush_kernel, seq_count), out_shape=jax....  1.53 us

profile of v7, /device:TPU:1, one launch (start us, length us, event | category | flops | bytes accessed | tf_op | source)
XLA Modules:
  0.0 57.8 jit_solution(5281085966099223310)
XLA Ops:
  0.0 56.3 %fused.1 = (bf16[2,32,256,128]{3,2,1,0:T(8,128)(2,1)S(1)}, s32[36,1,128]{2,1,0:T(1,128)S(1)}, s32[36,1,128]{2,1,0:T(1,128)S(1)}) custom-call(bf16[256,5120]{1,0:T(8,128)(2,1)} %key_ref.1, bf16[256,5120]{1,0:T(8,128)(2,1)} %value_ref.1, bf16[256,5120]{1,0:T(8,128)(2,1)} %query_hbm.1, s32[20,512]{1,0:T(8,128)} %perm_hbm.1, s32[20,4,64]{2,1,0:T(4,128)} %mask_hbm.1), custom_call_target="tpu_custom_call" | custom-call | tf_op jit(solution)/shard_map/fused/pallas_call | solution.py:651
  56.3 1.5 %flush.1 = bf16[256,5120]{1,0:T(8,128)(2,1)} custom-call(bf16[2,32,256,128]{3,2,1,0:T(8,128)(2,1)S(1)} %get-tuple-element.8.stage_ref, s32[36,1,128]{2,1,0:T(1,128)S(1)} %get-tuple-element.9.tab_ref, s32[36,1,128]{2,1,0:T(1,128)S(1)} %get-tuple-element.10.far_tab_ref), custom_call_target="tpu_custom_call" | custom-call | tf_op jit(solution)/shard_map/flush/pallas_call | solution.py:680
